TPU v7x, 256 devices: a whole 4x4x8 slice. The times are simulated.
256 devices in a mesh: group: 8 (over x, core), prompt: 32 (over z, y).
Axes of the slice: x: 4, y: 4, z: 8, core: 2. Of those that a mesh axis runs over, the one named last changes fastest.
Arguments:
- queries: bfloat16 [32, 8, 64, 3072], P('prompt', 'group'), may hold values from -48 to 48
- fresh_latent: bfloat16 [32, 8, 64, 576], P('prompt', 'group'), may hold values from -6 to 6
- latent_cache: bfloat16 [32, 8, 512, 576], P('prompt', 'group'), may hold values from -48 to 48
- selected: int32 [32, 8, 64], P('prompt', 'group'), may hold values from 0 to 511, as said below
- position: int32 [32, 8], P('prompt'), may hold values from 0 to 7, each once within a row
- latent_gain: bfloat16 [512], replicated, may hold values from 0.099609375 to 1.8984375
- kv_up: bfloat16 [512, 4096], P('prompt'), may hold values from -0.25 to 0.25
- out_weight: bfloat16 [2048, 2048], P('prompt'), may hold values from -0.125 to 0.125
Outputs:
- attended: bfloat16 [32, 8, 64, 2048], P('prompt', 'group')
- blended: bfloat16 [32, 8, 512, 576], P('prompt', 'group')
Inputs may be any that keep to these rules, and one draw needn't show every extreme that they name: `selected`: the 64 indices of a group are distinct and increasing.
All inputs are finite; a program needn't handle non-finite values.
Results may differ from a plain program's by a relative error of at most 0.011.
Values may be sent and summed in bfloat16 or wider, within the bound.
A program may use at most 128 MiB of HBM per device.

v0:
```python
import jax
import jax.numpy as jnp
from jax import lax
from jax.sharding import Mesh
from jax.sharding import PartitionSpec as P

D = 2048
H = 16
DN = 128
DR = 64
DV = 128
LAT = 512
PROMPT = ("prompt_0", "prompt_1")


def whole_of(array, axes, dim):
    whole = array
    for number in range(len(axes) - 1, -1, -1):
        whole = lax.all_gather(whole, axes[number], axis=dim, tiled=True)
    return whole


def rope_rotate(values, places):
    half = values.shape[-1] // 2
    freqs = 10000.0 ** (-jnp.arange(half, dtype=jnp.float32) / half)
    angles = places[..., None] * freqs
    cosine = jnp.cos(angles)
    sine = jnp.sin(angles)
    first = values[..., :half]
    second = values[..., half:]
    return jnp.concatenate([first * cosine - second * sine, second * cosine + first * sine], -1)


def prepare_rows(fresh, gain, places):
    latent = fresh[..., :LAT].astype(jnp.float32)
    factor = lax.rsqrt(jnp.mean(latent * latent, -1, keepdims=True) + 1e-06)
    normed = latent * factor * gain.astype(jnp.float32)
    turned = rope_rotate(fresh[..., LAT:].astype(jnp.float32), places)
    return jnp.concatenate([normed, turned], -1).astype(jnp.bfloat16)


def shards(queries, fresh_latent, latent_cache, selected, position, latent_gain, kv_up, out_weight):
    prompts, groups, picks, _ = queries.shape
    length = latent_cache.shape[2]
    first_group = lax.axis_index("group") * groups
    own_order = lax.dynamic_slice_in_dim(position, first_group, groups, 1)
    place_int = own_order[:, :, None] * length + selected
    places = place_int.astype(jnp.float32)
    fresh_rows = prepare_rows(fresh_latent, latent_gain, places)
    prompt_ids = jnp.arange(prompts, dtype=jnp.int32)[:, None, None]
    group_ids = jnp.arange(groups, dtype=jnp.int32)[None, :, None]
    blended = latent_cache.at[prompt_ids, group_ids, selected].set(fresh_rows)
    whole_kv = whole_of(kv_up, PROMPT, 0).reshape(LAT, H, DN + DV)
    shaped = queries.reshape(prompts, groups, picks, H, DN + DR)
    absorbed = jnp.einsum(
        "pcshd,lhd->pcshl", shaped[..., :DN], whole_kv[..., :DN], preferred_element_type=jnp.float32
    ).astype(jnp.bfloat16)
    turned = rope_rotate(shaped[..., DN:].astype(jnp.float32), places[..., None]).astype(
        jnp.bfloat16
    )
    rows = groups * picks
    query_vec = jnp.concatenate([absorbed, turned], -1).reshape(prompts, rows, H, LAT + DR)
    query_place = place_int.reshape(prompts, rows)
    scale = (DN + DR) ** (-0.5)
    offsets = jnp.arange(length, dtype=jnp.int32)

    def update(state, keys, key_place):
        peak, total, mixed = state
        allowed = (key_place[:, None, :] <= query_place[:, :, None])[:, :, None, :]
        scores = (
            jnp.einsum("pqhe,pke->pqhk", query_vec, keys, preferred_element_type=jnp.float32)
            * scale
        )
        block_peak = jnp.max(jnp.where(allowed, scores, -1e30), -1)
        new_peak = jnp.maximum(peak, block_peak)
        probs = jnp.where(allowed, jnp.exp(scores - new_peak[..., None]), 0.0)
        decay = jnp.exp(peak - new_peak)
        total = total * decay + jnp.sum(probs, -1)
        mixed = mixed * decay[..., None] + jnp.einsum(
            "pqhk,pkl->pqhl",
            probs.astype(jnp.bfloat16),
            keys[..., :LAT],
            preferred_element_type=jnp.float32,
        )
        return (new_peak, total, mixed)

    start_state = (
        jnp.full((prompts, rows, H), -1e30, jnp.float32),
        jnp.zeros((prompts, rows, H), jnp.float32),
        jnp.zeros((prompts, rows, H, LAT), jnp.float32),
    )
    piece = lax.all_gather(blended, "group", axis=1, tiled=True)

    def one_group(index, carry):
        keys = lax.dynamic_slice_in_dim(piece, index, 1, 1)[:, 0]
        order = lax.dynamic_slice_in_dim(position, index, 1, 1)
        key_place = order * length + offsets[None, :]
        needed = jnp.any(key_place[:, :1] <= jnp.max(query_place, -1, keepdims=True))
        return lax.cond(needed, lambda c: update(c, keys, key_place), lambda c: c, carry)

    peak, total, mixed = lax.fori_loop(0, piece.shape[1], one_group, start_state)
    latent_mix = (mixed / total[..., None]).astype(jnp.bfloat16)
    heads = jnp.einsum(
        "pqhl,lhv->pqhv", latent_mix, whole_kv[..., DN:], preferred_element_type=jnp.float32
    ).astype(jnp.bfloat16)
    heads = heads.reshape(prompts * rows, H * DV)
    whole_out = lax.all_gather(out_weight, PROMPT, axis=0, tiled=True)
    attended = jnp.dot(heads, whole_out, preferred_element_type=jnp.float32)
    return (attended.astype(jnp.bfloat16).reshape(prompts, groups, picks, D), blended)


def solution(mesh):
    split = Mesh(mesh.devices.reshape(mesh.shape["group"], 8, 4), ("group", "prompt_0", "prompt_1"))
    return jax.shard_map(
        shards,
        mesh=split,
        in_specs=(
            P(PROMPT, "group", None, None),
            P(PROMPT, "group", None, None),
            P(PROMPT, "group", None, None),
            P(PROMPT, "group", None),
            P(PROMPT, None),
            P(),
            P(PROMPT, None),
            P(PROMPT, None),
        ),
        out_specs=(P(PROMPT, "group", None, None), P(PROMPT, "group", None, None)),
        check_vma=False,
    )
```

profile of v0, /device:TPU:57, one launch (start us, length us, event | category | flops | bytes accessed | tf_op | source)
XLA Modules:
  0.0 239.9 jit_solution(15318648085517091847)
XLA Ops:
  7.2 10.8 %all_gather.13 = bf16[64,4096]{1,0:T(8,128)(2,1)} all-gather(bf16[16,4096]{1,0:T(8,128)(2,1)} %param.18), channel_id=1, replica_groups=mesh['group'=8,'prompt_0'=8,'prompt_1'=4] {'prompt_1'}, dimensions={0}, use_global_device_ids=true | all-gather | bytes 655360 | tf_op jit(solution)/shard_map/all_gather | solution.py:19
  18.2 0.8 slice.44
  19.0 1.2 fusion.52
  20.3 1.3 convert_bitcast_fusion
  21.9 1.4 copy.49
  23.6 1.3 scatter_custom_fusion
  24.9 0.8 copy-done.1
  27.2 1.1 copy.62
  29.4 46.8 %all-gather.5.cloned.1.call-done = bf16[512,4096]{1,0:T(8,128)(2,1)} async-done(((bf16[64,4096]{1,0:T(8,128)(2,1)}), bf16[512,4096]{1,0:T(8,128)(2,1)}) %all-gather.5.cloned.1.call-update) | async-done | bytes 4194320 | tf_op jit(solution)/shard_map/all_gather | solution.py:19
  76.2 6.5 %copy.53 = bf16[512,4096]{0,1:T(8,128)(2,1)} copy(bf16[512,4096]{1,0:T(8,128)(2,1)} %all-gather.5.cloned.1.call-done) | data formatting | bytes 8388608 | tf_op jit(solution)/shard_map/all_gather | solution.py:19
  82.7 2.0 fusion.20
  84.8 1.3 maximum_bitcast_fusion
  86.1 31.9 %all-gather.9.cloned.1.call-done = bf16[4096,576]{1,0:T(8,128)(2,1)} async-done(((bf16[512,576]{1,0:T(8,128)(2,1)}), bf16[4096,576]{1,0:T(8,128)(2,1)}) %all-gather.9.cloned.1.call-update) | async-done | bytes 4718608 | tf_op jit(solution)/shard_map/all_gather | solution.py:92
  118.0 7.7 %copy.57 = bf16[1,8,512,576]{2,3,1,0:T(8,128)(2,1)} copy(bf16[1,8,512,576]{3,2,1,0:T(8,128)(2,1)} %bitcast.103) | data formatting | bytes 9437184
  126.3 98.4 %while.20 = (s32[]{:T(128)}, f32[1,64,16]{1,2,0:T(8,128)S(1)}, f32[1,64,16]{1,2,0:T(8,128)S(1)}, f32[1,64,16,512]{3,2,1,0:T(8,128)S(1)}, s32[1,8]{1,0:T(1,128)S(...) while((s32[]{:T(128)}, f32[1,64,16]{1,2,0:T(8,128)S(1)}, ...), condition=%wide.region_8.9_spmd.clone, body=%wide.region_3.8_spmd.clone.sunk | while | flops 1146129920 | bytes 17670692 | solution.py:101
  129.5 9.0 %conditional.3 = ((f32[1,64,16]{1,2,0:T(8,128)S(1)}, f32[1,64,16]{1,2,0:T(8,128)S(1)}, f32[1,64,16,512]{3,2,1,0:T(8,128)S(1)})) conditional(s32[]{:T(128)} %bitcast.97, (f32[1,64,16]{1,2,0:T(8,128)S(1)}, f32[1,64,16]{1,2,0:T(8,128)S(1)}, f32[1,64,16,512]{3,2,1,0:T(8,128)S(1)}) %tuple.70, (s32[1,512]{1,0:T(1,128)S(1)}, s32[1,1,64]{2,1,0:T(1,128)S(1)}, ...), branch_computations={%region_4.0_spmd, %region_5.7_spmd} | conditional | flops 1146129408 | bytes 17668416 | solution.py:99
  129.6 1.1 constant_dynamic-slice_fusion
  130.8 2.5 %fusion.2 = (f32[64,16]{0,1:T(8,128)S(1)}, f32[512,64,16]{0,1,2:T(8,128)S(1)}) fusion(pred[64,512]{1,0:T(8,128)(4,1)S(1)} %broadcast_compare_fusion, bf16[1,64,16,576]{3,1,2,0:T(8,128)(2,1)} %get-tuple-element.279, bf16[1,1,512,576]{2,3,1,0:T(8,128)(2,1)S(1)} %constant_dynamic-slice_fusion), kind=kOutput, calls=%fused_computation.5 | convolution fusion | flops 605551616 | bytes 3903488 | tf_op jit(solution)/shard_map/while/body/eval_jaxpr/cond/branch_1_fun/pqhe,pke->pqhk/dot_general | solution.py:71
  133.3 0.7 fusion.5
  134.1 2.2 copy.47
  136.3 2.2 bitcast_add_fusion
  141.8 9.1 %conditional.3 = ((f32[1,64,16]{1,2,0:T(8,128)S(1)}, f32[1,64,16]{1,2,0:T(8,128)S(1)}, f32[1,64,16,512]{3,2,1,0:T(8,128)S(1)})) conditional(s32[]{:T(128)} %bitcast.97, (f32[1,64,16]{1,2,0:T(8,128)S(1)}, f32[1,64,16]{1,2,0:T(8,128)S(1)}, f32[1,64,16,512]{3,2,1,0:T(8,128)S(1)}) %tuple.70, (s32[1,512]{1,0:T(1,128)S(1)}, s32[1,1,64]{2,1,0:T(1,128)S(1)}, ...), branch_computations={%region_4.0_spmd, %region_5.7_spmd} | conditional | flops 1146129408 | bytes 17668416 | solution.py:99
  141.8 1.1 constant_dynamic-slice_fusion
  143.1 2.5 %fusion.2 = (f32[64,16]{0,1:T(8,128)S(1)}, f32[512,64,16]{0,1,2:T(8,128)S(1)}) fusion(pred[64,512]{1,0:T(8,128)(4,1)S(1)} %broadcast_compare_fusion, bf16[1,64,16,576]{3,1,2,0:T(8,128)(2,1)} %get-tuple-element.279, bf16[1,1,512,576]{2,3,1,0:T(8,128)(2,1)S(1)} %constant_dynamic-slice_fusion), kind=kOutput, calls=%fused_computation.5 | convolution fusion | flops 605551616 | bytes 3903488 | tf_op jit(solution)/shard_map/while/body/eval_jaxpr/cond/branch_1_fun/pqhe,pke->pqhk/dot_general | solution.py:71
  145.6 0.7 fusion.5
  146.4 2.2 copy.47
  148.7 2.2 bitcast_add_fusion
  154.1 9.0 %conditional.3 = ((f32[1,64,16]{1,2,0:T(8,128)S(1)}, f32[1,64,16]{1,2,0:T(8,128)S(1)}, f32[1,64,16,512]{3,2,1,0:T(8,128)S(1)})) conditional(s32[]{:T(128)} %bitcast.97, (f32[1,64,16]{1,2,0:T(8,128)S(1)}, f32[1,64,16]{1,2,0:T(8,128)S(1)}, f32[1,64,16,512]{3,2,1,0:T(8,128)S(1)}) %tuple.70, (s32[1,512]{1,0:T(1,128)S(1)}, s32[1,1,64]{2,1,0:T(1,128)S(1)}, ...), branch_computations={%region_4.0_spmd, %region_5.7_spmd} | conditional | flops 1146129408 | bytes 17668416 | solution.py:99
  154.1 1.1 constant_dynamic-slice_fusion
  155.4 2.5 %fusion.2 = (f32[64,16]{0,1:T(8,128)S(1)}, f32[512,64,16]{0,1,2:T(8,128)S(1)}) fusion(pred[64,512]{1,0:T(8,128)(4,1)S(1)} %broadcast_compare_fusion, bf16[1,64,16,576]{3,1,2,0:T(8,128)(2,1)} %get-tuple-element.279, bf16[1,1,512,576]{2,3,1,0:T(8,128)(2,1)S(1)} %constant_dynamic-slice_fusion), kind=kOutput, calls=%fused_computation.5 | convolution fusion | flops 605551616 | bytes 3903488 | tf_op jit(solution)/shard_map/while/body/eval_jaxpr/cond/branch_1_fun/pqhe,pke->pqhk/dot_general | solution.py:71
  157.9 0.7 fusion.5
  158.7 2.2 copy.47
  160.9 2.2 bitcast_add_fusion
  166.4 9.2 %conditional.3 = ((f32[1,64,16]{1,2,0:T(8,128)S(1)}, f32[1,64,16]{1,2,0:T(8,128)S(1)}, f32[1,64,16,512]{3,2,1,0:T(8,128)S(1)})) conditional(s32[]{:T(128)} %bitcast.97, (f32[1,64,16]{1,2,0:T(8,128)S(1)}, f32[1,64,16]{1,2,0:T(8,128)S(1)}, f32[1,64,16,512]{3,2,1,0:T(8,128)S(1)}) %tuple.70, (s32[1,512]{1,0:T(1,128)S(1)}, s32[1,1,64]{2,1,0:T(1,128)S(1)}, ...), branch_computations={%region_4.0_spmd, %region_5.7_spmd} | conditional | flops 1146129408 | bytes 17668416 | solution.py:99
  166.4 1.1 constant_dynamic-slice_fusion
  167.6 2.5 %fusion.2 = (f32[64,16]{0,1:T(8,128)S(1)}, f32[512,64,16]{0,1,2:T(8,128)S(1)}) fusion(pred[64,512]{1,0:T(8,128)(4,1)S(1)} %broadcast_compare_fusion, bf16[1,64,16,576]{3,1,2,0:T(8,128)(2,1)} %get-tuple-element.279, bf16[1,1,512,576]{2,3,1,0:T(8,128)(2,1)S(1)} %constant_dynamic-slice_fusion), kind=kOutput, calls=%fused_computation.5 | convolution fusion | flops 605551616 | bytes 3903488 | tf_op jit(solution)/shard_map/while/body/eval_jaxpr/cond/branch_1_fun/pqhe,pke->pqhk/dot_general | solution.py:71
  170.2 0.7 fusion.5
  171.0 2.3 copy.47
  173.3 2.2 bitcast_add_fusion
  178.8 9.1 %conditional.3 = ((f32[1,64,16]{1,2,0:T(8,128)S(1)}, f32[1,64,16]{1,2,0:T(8,128)S(1)}, f32[1,64,16,512]{3,2,1,0:T(8,128)S(1)})) conditional(s32[]{:T(128)} %bitcast.97, (f32[1,64,16]{1,2,0:T(8,128)S(1)}, f32[1,64,16]{1,2,0:T(8,128)S(1)}, f32[1,64,16,512]{3,2,1,0:T(8,128)S(1)}) %tuple.70, (s32[1,512]{1,0:T(1,128)S(1)}, s32[1,1,64]{2,1,0:T(1,128)S(1)}, ...), branch_computations={%region_4.0_spmd, %region_5.7_spmd} | conditional | flops 1146129408 | bytes 17668416 | solution.py:99
  178.8 1.1 constant_dynamic-slice_fusion
  180.0 2.5 %fusion.2 = (f32[64,16]{0,1:T(8,128)S(1)}, f32[512,64,16]{0,1,2:T(8,128)S(1)}) fusion(pred[64,512]{1,0:T(8,128)(4,1)S(1)} %broadcast_compare_fusion, bf16[1,64,16,576]{3,1,2,0:T(8,128)(2,1)} %get-tuple-element.279, bf16[1,1,512,576]{2,3,1,0:T(8,128)(2,1)S(1)} %constant_dynamic-slice_fusion), kind=kOutput, calls=%fused_computation.5 | convolution fusion | flops 605551616 | bytes 3903488 | tf_op jit(solution)/shard_map/while/body/eval_jaxpr/cond/branch_1_fun/pqhe,pke->pqhk/dot_general | solution.py:71
  182.6 0.7 fusion.5
  183.4 2.2 copy.47
  185.6 2.2 bitcast_add_fusion
  191.1 9.1 %conditional.3 = ((f32[1,64,16]{1,2,0:T(8,128)S(1)}, f32[1,64,16]{1,2,0:T(8,128)S(1)}, f32[1,64,16,512]{3,2,1,0:T(8,128)S(1)})) conditional(s32[]{:T(128)} %bitcast.97, (f32[1,64,16]{1,2,0:T(8,128)S(1)}, f32[1,64,16]{1,2,0:T(8,128)S(1)}, f32[1,64,16,512]{3,2,1,0:T(8,128)S(1)}) %tuple.70, (s32[1,512]{1,0:T(1,128)S(1)}, s32[1,1,64]{2,1,0:T(1,128)S(1)}, ...), branch_computations={%region_4.0_spmd, %region_5.7_spmd} | conditional | flops 1146129408 | bytes 17668416 | solution.py:99
  191.1 1.1 constant_dynamic-slice_fusion
  192.3 2.6 %fusion.2 = (f32[64,16]{0,1:T(8,128)S(1)}, f32[512,64,16]{0,1,2:T(8,128)S(1)}) fusion(pred[64,512]{1,0:T(8,128)(4,1)S(1)} %broadcast_compare_fusion, bf16[1,64,16,576]{3,1,2,0:T(8,128)(2,1)} %get-tuple-element.279, bf16[1,1,512,576]{2,3,1,0:T(8,128)(2,1)S(1)} %constant_dynamic-slice_fusion), kind=kOutput, calls=%fused_computation.5 | convolution fusion | flops 605551616 | bytes 3903488 | tf_op jit(solution)/shard_map/while/body/eval_jaxpr/cond/branch_1_fun/pqhe,pke->pqhk/dot_general | solution.py:71
  194.9 0.7 fusion.5
  195.7 2.2 copy.47
  197.9 2.2 bitcast_add_fusion
  203.4 9.1 %conditional.3 = ((f32[1,64,16]{1,2,0:T(8,128)S(1)}, f32[1,64,16]{1,2,0:T(8,128)S(1)}, f32[1,64,16,512]{3,2,1,0:T(8,128)S(1)})) conditional(s32[]{:T(128)} %bitcast.97, (f32[1,64,16]{1,2,0:T(8,128)S(1)}, f32[1,64,16]{1,2,0:T(8,128)S(1)}, f32[1,64,16,512]{3,2,1,0:T(8,128)S(1)}) %tuple.70, (s32[1,512]{1,0:T(1,128)S(1)}, s32[1,1,64]{2,1,0:T(1,128)S(1)}, ...), branch_computations={%region_4.0_spmd, %region_5.7_spmd} | conditional | flops 1146129408 | bytes 17668416 | solution.py:99
  203.4 1.1 constant_dynamic-slice_fusion
  204.7 2.5 %fusion.2 = (f32[64,16]{0,1:T(8,128)S(1)}, f32[512,64,16]{0,1,2:T(8,128)S(1)}) fusion(pred[64,512]{1,0:T(8,128)(4,1)S(1)} %broadcast_compare_fusion, bf16[1,64,16,576]{3,1,2,0:T(8,128)(2,1)} %get-tuple-element.279, bf16[1,1,512,576]{2,3,1,0:T(8,128)(2,1)S(1)} %constant_dynamic-slice_fusion), kind=kOutput, calls=%fused_computation.5 | convolution fusion | flops 605551616 | bytes 3903488 | tf_op jit(solution)/shard_map/while/body/eval_jaxpr/cond/branch_1_fun/pqhe,pke->pqhk/dot_general | solution.py:71
  207.2 0.7 fusion.5
  208.0 2.2 copy.47
  210.2 2.2 bitcast_add_fusion
  215.7 9.0 %conditional.3 = ((f32[1,64,16]{1,2,0:T(8,128)S(1)}, f32[1,64,16]{1,2,0:T(8,128)S(1)}, f32[1,64,16,512]{3,2,1,0:T(8,128)S(1)})) conditional(s32[]{:T(128)} %bitcast.97, (f32[1,64,16]{1,2,0:T(8,128)S(1)}, f32[1,64,16]{1,2,0:T(8,128)S(1)}, f32[1,64,16,512]{3,2,1,0:T(8,128)S(1)}) %tuple.70, (s32[1,512]{1,0:T(1,128)S(1)}, s32[1,1,64]{2,1,0:T(1,128)S(1)}, ...), branch_computations={%region_4.0_spmd, %region_5.7_spmd} | conditional | flops 1146129408 | bytes 17668416 | solution.py:99
  215.7 1.1 constant_dynamic-slice_fusion
  216.9 2.5 %fusion.2 = (f32[64,16]{0,1:T(8,128)S(1)}, f32[512,64,16]{0,1,2:T(8,128)S(1)}) fusion(pred[64,512]{1,0:T(8,128)(4,1)S(1)} %broadcast_compare_fusion, bf16[1,64,16,576]{3,1,2,0:T(8,128)(2,1)} %get-tuple-element.279, bf16[1,1,512,576]{2,3,1,0:T(8,128)(2,1)S(1)} %constant_dynamic-slice_fusion), kind=kOutput, calls=%fused_computation.5 | convolution fusion | flops 605551616 | bytes 3903488 | tf_op jit(solution)/shard_map/while/body/eval_jaxpr/cond/branch_1_fun/pqhe,pke->pqhk/dot_general | solution.py:71
  220.3 2.2 copy.47
  222.5 2.2 bitcast_add_fusion
  225.1 2.4 %fusion.26 = bf16[1,64,16,128]{3,1,2,0:T(8,128)(2,1)S(1)} fusion(bf16[512,16,256]{0,2,1:T(8,128)(2,1)} %bitcast.100, bf16[64,16,512]{2,1,0:T(8,128)(2,1)S(1)} %fusion.30), kind=kOutput, calls=%fused_computation.34 | convolution fusion | flops 134348800 | bytes 3407872 | tf_op jit(solution)/shard_map/pqhl,lhv->pqhv/dot_general | solution.py:103
  227.7 5.7 %fusion.12 = bf16[1,1,64,2048]{3,2,1,0:T(8,128)(2,1)} fusion(bf16[2048,2048]{1,0:T(8,128)(2,1)} %all-gather.7.cloned.1.call-done, bf16[8,8,16,128]{3,2,1,0:T(8,128)(2,1)S(1)} %bitcast.105), kind=kOutput, calls=%fused_computation.24 | convolution fusion | flops 537001984 | bytes 8912896 | tf_op jit(solution)/shard_map/dot_general | solution.py:108
  (127 shorter events, 22.3 us)
Async XLA Ops:
  7.2 16.2 %copy-start.5 = (bf16[1,1,64,576]{3,2,1,0:T(8,128)(2,1)S(1)}, bf16[1,1,64,576]{3,2,1,0:T(8,128)(2,1)}, u32[]{:S(2)}) copy-start(bf16[1,1,64,576]{3,2,1,0:T(8,128)(2,1)} %param.13) | copy-start | bytes 221188
  7.2 16.1 %copy-start.6 = (bf16[512]{0:T(512)(128)(2,1)S(1)}, bf16[512]{0:T(512)(128)(2,1)}, u32[]{:S(2)}) copy-start(bf16[512]{0:T(512)(128)(2,1)} %param.17) | copy-start | bytes 3076
  7.2 69.0 %all-gather.5.cloned.1.call-start = ((), (), s32[]{:S(2)}) async-start(), calls=%async_computation | async-start | bytes 4718592 | tf_op jit(solution)/shard_map/all_gather | solution.py:19
  18.1 8.4 %copy-start.4 = (bf16[1,1,64,3072]{3,2,1,0:T(8,128)(2,1)S(1)}, bf16[1,1,64,3072]{3,2,1,0:T(8,128)(2,1)}, u32[]{:S(2)}) copy-start(bf16[1,1,64,3072]{3,2,1,0:T(8,128)(2,1)} %param.12) | copy-start | bytes 1179652
  18.1 99.9 %all-gather.9.cloned.1.call-start = ((), (), s32[]{:S(2)}) async-start(), calls=%async_computation.2 | async-start | bytes 5898240 | tf_op jit(solution)/shard_map/all_gather | solution.py:92
  24.9 0.8 copy-start.1
  25.8 1.4 copy-start.2
  25.8 201.9 %all-gather.7.cloned.1.call-start = ((), (), s32[]{:S(2)}) async-start(), calls=%async_computation.1 | async-start | bytes 8650752 | tf_op jit(solution)/shard_map/all_gather | solution.py:107
  27.1 2.3 copy-start.3
  76.2 6.5 %slice-start = ((bf16[1,1,64,16,192]{4,3,2,1,0:T(8,128)(2,1)}), bf16[1,1,64,16,128]{4,3,2,1,0:T(8,128)(2,1)S(1)}, s32[]{:S(2)}) async-start(bf16[1,1,64,16,192]{4,3,2,1,0:T(8,128)(2,1)} %copy-done.3), calls=%async_computation.3 | async-start | bytes 524288 | tf_op jit(solution)/shard_map/slice | solution.py:56
  125.7 0.7 copy-start.7
  130.7 2.6 %copy-start = (bf16[1,1,512,576]{2,3,1,0:T(8,128)(2,1)}, bf16[1,1,512,576]{2,3,1,0:T(8,128)(2,1)S(1)}, u32[]{:S(2)}) copy-start(bf16[1,1,512,576]{2,3,1,0:T(8,128)(2,1)S(1)} %constant_dynamic-slice_fusion) | copy-start | bytes 1769476 | tf_op jit(solution)/shard_map/while/body/eval_jaxpr/cond
  143.0 2.7 %copy-start = (bf16[1,1,512,576]{2,3,1,0:T(8,128)(2,1)}, bf16[1,1,512,576]{2,3,1,0:T(8,128)(2,1)S(1)}, u32[]{:S(2)}) copy-start(bf16[1,1,512,576]{2,3,1,0:T(8,128)(2,1)S(1)} %constant_dynamic-slice_fusion) | copy-start | bytes 1769476 | tf_op jit(solution)/shard_map/while/body/eval_jaxpr/cond
  155.3 2.6 %copy-start = (bf16[1,1,512,576]{2,3,1,0:T(8,128)(2,1)}, bf16[1,1,512,576]{2,3,1,0:T(8,128)(2,1)S(1)}, u32[]{:S(2)}) copy-start(bf16[1,1,512,576]{2,3,1,0:T(8,128)(2,1)S(1)} %constant_dynamic-slice_fusion) | copy-start | bytes 1769476 | tf_op jit(solution)/shard_map/while/body/eval_jaxpr/cond
  167.5 2.6 %copy-start = (bf16[1,1,512,576]{2,3,1,0:T(8,128)(2,1)}, bf16[1,1,512,576]{2,3,1,0:T(8,128)(2,1)S(1)}, u32[]{:S(2)}) copy-start(bf16[1,1,512,576]{2,3,1,0:T(8,128)(2,1)S(1)} %constant_dynamic-slice_fusion) | copy-start | bytes 1769476 | tf_op jit(solution)/shard_map/while/body/eval_jaxpr/cond
  179.9 2.6 %copy-start = (bf16[1,1,512,576]{2,3,1,0:T(8,128)(2,1)}, bf16[1,1,512,576]{2,3,1,0:T(8,128)(2,1)S(1)}, u32[]{:S(2)}) copy-start(bf16[1,1,512,576]{2,3,1,0:T(8,128)(2,1)S(1)} %constant_dynamic-slice_fusion) | copy-start | bytes 1769476 | tf_op jit(solution)/shard_map/while/body/eval_jaxpr/cond
  192.2 2.7 %copy-start = (bf16[1,1,512,576]{2,3,1,0:T(8,128)(2,1)}, bf16[1,1,512,576]{2,3,1,0:T(8,128)(2,1)S(1)}, u32[]{:S(2)}) copy-start(bf16[1,1,512,576]{2,3,1,0:T(8,128)(2,1)S(1)} %constant_dynamic-slice_fusion) | copy-start | bytes 1769476 | tf_op jit(solution)/shard_map/while/body/eval_jaxpr/cond
  204.6 2.6 %copy-start = (bf16[1,1,512,576]{2,3,1,0:T(8,128)(2,1)}, bf16[1,1,512,576]{2,3,1,0:T(8,128)(2,1)S(1)}, u32[]{:S(2)}) copy-start(bf16[1,1,512,576]{2,3,1,0:T(8,128)(2,1)S(1)} %constant_dynamic-slice_fusion) | copy-start | bytes 1769476 | tf_op jit(solution)/shard_map/while/body/eval_jaxpr/cond
  216.8 2.6 %copy-start = (bf16[1,1,512,576]{2,3,1,0:T(8,128)(2,1)}, bf16[1,1,512,576]{2,3,1,0:T(8,128)(2,1)S(1)}, u32[]{:S(2)}) copy-start(bf16[1,1,512,576]{2,3,1,0:T(8,128)(2,1)S(1)} %constant_dynamic-slice_fusion) | copy-start | bytes 1769476 | tf_op jit(solution)/shard_map/while/body/eval_jaxpr/cond
Sparse Core Ops, SparseCore 0:
  18.2 57.9 all-gather.4
  78.0 39.9 all-gather.8
  120.6 93.4 all-gather.6
where the time goes:
time: 242 us; the launch traced here: 240 us
  waiting for transfers between devices  79.4 us (33%)
  local copies, waits for them, and re-layouts  52.4 us (22%)
  matrix products  48.2 us (20%)
  other arithmetic  24.2 us (10%)
  between operations  14 us (6%)
  blocking collectives  10.8 us (4%)
  loops' own time  10.8 us (4%)
    all_gather x1, waiting for transfers between devices, whole_of(): whole = lax.all_gather(whole, axes[number], axis=dim, tiled=True)  46.8 us
    all_gather x1, waiting for transfers between devices, shards(): piece = lax.all_gather(blended, 'group', axis=1, tiled=True)  31.9 us
    dynamic_slice x16, local copies, waits for them, and re-layouts, one_group(): keys = lax.dynamic_slice_in_dim(piece, index, 1, 1)[:, 0]  26.8 us
    dot_general x8, matrix products, update(): jnp.einsum('pqhe,pke->pqhk', query_vec, keys, preferred_element_type=jnp....  20.2 us
    dot_general x8, matrix products, update(): jnp.einsum('pqhk,pkl->pqhl', probs.astype(jnp.bfloat16), keys[..., :LAT],...  17.9 us
    unnamed x18, local copies, waits for them, and re-layouts  11.4 us
    all_gather x1, blocking collectives, whole_of(): whole = lax.all_gather(whole, axes[number], axis=dim, tiled=True)  10.8 us
    another operation x1, loops' own time, shards(): lax.fori_loop(0, piece.shape[1], one_group, start_state)  10.2 us
  transfers between devices with their start and end apart: 3, of which 2 were waited for; matrix products, arithmetic and copies ran while one was open for 49% of the time, Pallas kernels for 0%

commit v1 on v0

--- a/solution.py
+++ b/solution.py
@@ -11,6 +11,12 @@
 DV = 128
 LAT = 512
 PROMPT = ("prompt_0", "prompt_1")
+
+
+def recover_roots(my_data, axis_k):
+    carry_in = jnp.stack(tuple((my_data for _ in range(jax.lax.axis_size("group")))))
+    big = jnp.concatenate(jax.lax.all_to_all(carry_in, "group", 0, 0), axis_k)
+    return big
 
 
 def whole_of(array, axes, dim):
@@ -89,7 +95,7 @@
         jnp.zeros((prompts, rows, H), jnp.float32),
         jnp.zeros((prompts, rows, H, LAT), jnp.float32),
     )
-    piece = lax.all_gather(blended, "group", axis=1, tiled=True)
+    piece = recover_roots(blended, 1)
 
     def one_group(index, carry):
         keys = lax.dynamic_slice_in_dim(piece, index, 1, 1)[:, 0]

time: 242 us -> 207 us (0.86)
  waiting for transfers between devices: 79.4 us -> 42.3 us
  starting transfers between devices: 0.12 us -> 8.3 us
  local copies, waits for them, and re-layouts: 52.4 us -> 45.1 us
    all_gather x1 -> x0, waiting for transfers between devices: 31.9 us -> none  [shards(): piece = lax.all_gather(blended, 'group', axis=1, tiled=True)]
    all_gather x1, waiting for transfers between devices: 46.8 us -> 36.6 us  [whole_of(): whole = lax.all_gather(whole, axes[number], axis=dim, tiled=True)]
    unnamed x18 -> x13, local copies, waits for them, and re-layouts: 11.4 us -> 2.54 us
    all_to_all x0 -> x1, starting transfers between devices: none -> 8.22 us  [recover_roots(): big = jnp.concatenate(jax.lax.all_to_all(carry_in, 'group', 0, 0), axis_k)]
    all_to_all x0 -> x1, waiting for transfers between devices: none -> 4.99 us  [recover_roots(): big = jnp.concatenate(jax.lax.all_to_all(carry_in, 'group', 0, 0), axis_k)]
    another operation x2 -> x3, local copies, waits for them, and re-layouts: 0.19 us -> 2.71 us  [the longest x1 2.52 us: recover_roots(): jnp.stack(tuple((my_data for _ in range(jax.lax.axis_size('group')))))]
  transfers between devices with their start and end apart: 3 -> 3, of which waited for: 2 -> 2; matrix products, arithmetic and copies ran while one was open for 49% -> 54% of each run, Pallas kernels for 0% -> 0%
where the time goes in v1:
time: 207 us; the launch traced here: 203 us
  matrix products  48.1 us (23%)
  local copies, waits for them, and re-layouts  45.1 us (22%)
  waiting for transfers between devices  42.3 us (20%)
  other arithmetic  23.1 us (11%)
  between operations  14.3 us (7%)
  loops' own time  11.3 us (5%)
  blocking collectives  10.8 us (5%)
  starting transfers between devices  8.3 us (4%)
    all_gather x1, waiting for transfers between devices, whole_of(): whole = lax.all_gather(whole, axes[number], axis=dim, tiled=True)  36.6 us
    dynamic_slice x16, local copies, waits for them, and re-layouts, one_group(): keys = lax.dynamic_slice_in_dim(piece, index, 1, 1)[:, 0]  26.3 us
    dot_general x8, matrix products, update(): jnp.einsum('pqhe,pke->pqhk', query_vec, keys, preferred_element_type=jnp....  20.2 us
    dot_general x8, matrix products, update(): jnp.einsum('pqhk,pkl->pqhl', probs.astype(jnp.bfloat16), keys[..., :LAT],...  17.8 us
    all_gather x1, blocking collectives, whole_of(): whole = lax.all_gather(whole, axes[number], axis=dim, tiled=True)  10.8 us
    another operation x1, loops' own time, shards(): lax.fori_loop(0, piece.shape[1], one_group, start_state)  10.7 us
    all_to_all x1, starting transfers between devices, recover_roots(): big = jnp.concatenate(jax.lax.all_to_all(carry_in, 'group', 0, 0), axis_k)  8.22 us
    all_gather x1, local copies, waits for them, and re-layouts, whole_of(): whole = lax.all_gather(whole, axes[number], axis=dim, tiled=True)  6.52 us
  transfers between devices with their start and end apart: 3, of which 2 were waited for; matrix products, arithmetic and copies ran while one was open for 54% of the time, Pallas kernels for 0%

profile of v1, /device:TPU:57, one launch (start us, length us, event | category | flops | bytes accessed | tf_op | source)
XLA Modules:
  0.0 203.4 jit_solution(1903891036483067966)
XLA Ops:
  7.2 10.8 %all_gather.9 = bf16[64,4096]{1,0:T(8,128)(2,1)} all-gather(bf16[16,4096]{1,0:T(8,128)(2,1)} %param.18), channel_id=1, replica_groups=mesh['group'=8,'prompt_0'=8,'prompt_1'=4] {'prompt_1'}, dimensions={0}, use_global_device_ids=true | all-gather | bytes 655360 | tf_op jit(solution)/shard_map/all_gather | solution.py:25
  18.9 0.7 slice.44
  19.7 1.2 fusion.52
  20.9 1.3 convert_bitcast_fusion
  22.6 1.4 copy.48
  24.2 1.3 scatter_custom_fusion
  25.8 2.5 %stack.2 = bf16[8,1,1,512,576]{3,4,2,1,0:T(8,128)(2,1)} broadcast(bf16[512,576]{0,1:T(8,128)(2,1)S(1)} %copy.52), dimensions={3,4} | broadcast | bytes 5308416 | tf_op jit(solution)/shard_map/stack | solution.py:17
  28.3 8.2 %all-to-all-start = ((bf16[8,1,1,512,576]{3,4,2,1,0:T(8,128)(2,1)}), bf16[8,1,1,512,576]{3,4,2,1,0:T(8,128)(2,1)}, u32[]{:S(2)}, u32[]{:S(2)}) async-start(bf16[8,1,1,512,576]{3,4,2,1,0:T(8,128)(2,1)} %stack.2), calls=%async_computation | async-start | bytes 9437184 | tf_op jit(solution)/shard_map/all_to_all | solution.py:18
  37.2 1.1 copy.61
  38.3 0.7 reduce_max.22
  39.5 36.6 %all-gather.3.cloned.1.call-done = bf16[512,4096]{1,0:T(8,128)(2,1)} async-done(((bf16[64,4096]{1,0:T(8,128)(2,1)}), bf16[512,4096]{1,0:T(8,128)(2,1)}) %all-gather.3.cloned.1.call-update) | async-done | bytes 4194320 | tf_op jit(solution)/shard_map/all_gather | solution.py:25
  76.1 6.5 %copy.53 = bf16[512,4096]{0,1:T(8,128)(2,1)} copy(bf16[512,4096]{1,0:T(8,128)(2,1)} %all-gather.3.cloned.1.call-done) | data formatting | bytes 8388608 | tf_op jit(solution)/shard_map/all_gather | solution.py:25
  82.6 2.0 fusion.20
  84.7 1.3 maximum_bitcast_fusion
  86.0 5.0 %all-to-all-done = bf16[8,1,1,512,576]{3,4,2,1,0:T(8,128)(2,1)} async-done(((bf16[8,1,1,512,576]{3,4,2,1,0:T(8,128)(2,1)}), bf16[8,1,1,512,576]{3,4,2,1,0:T(8,128)(2,1)}, u32[]{:S(2)}, u32[]{:S(2)}) %all-to-all-start) | async-done | bytes 4718624 | tf_op jit(solution)/shard_map/all_to_all | solution.py:18
  91.3 96.7 %while.20 = (s32[]{:T(128)}, f32[1,64,16]{1,2,0:T(8,128)S(1)}, f32[1,64,16]{1,2,0:T(8,128)S(1)}, f32[1,64,16,512]{3,2,1,0:T(8,128)S(1)}, s32[1,8]{1,0:T(1,128)S(...) while((s32[]{:T(128)}, f32[1,64,16]{1,2,0:T(8,128)S(1)}, ...), condition=%wide.region_8.9_spmd.clone, body=%wide.region_3.8_spmd.clone.sunk | while | flops 1146129920 | bytes 17670692 | solution.py:107
  94.3 9.0 %conditional.3 = ((f32[1,64,16]{1,2,0:T(8,128)S(1)}, f32[1,64,16]{1,2,0:T(8,128)S(1)}, f32[1,64,16,512]{3,2,1,0:T(8,128)S(1)})) conditional(s32[]{:T(128)} %bitcast.97, (f32[1,64,16]{1,2,0:T(8,128)S(1)}, f32[1,64,16]{1,2,0:T(8,128)S(1)}, f32[1,64,16,512]{3,2,1,0:T(8,128)S(1)}) %tuple.66, (s32[1,512]{1,0:T(1,128)S(1)}, s32[1,1,64]{2,1,0:T(1,128)S(1)}, ...), branch_computations={%region_4.0_spmd, %region_5.7_spmd} | conditional | flops 1146129408 | bytes 17668416 | solution.py:105
  94.4 1.1 constant_dynamic-slice_fusion
  95.6 2.6 %fusion.2 = (f32[64,16]{0,1:T(8,128)S(1)}, f32[512,64,16]{0,1,2:T(8,128)S(1)}) fusion(pred[64,512]{1,0:T(8,128)(4,1)S(1)} %broadcast_compare_fusion, bf16[1,64,16,576]{3,1,2,0:T(8,128)(2,1)} %get-tuple-element.279, bf16[1,1,512,576]{2,3,1,0:T(8,128)(2,1)S(1)} %constant_dynamic-slice_fusion), kind=kOutput, calls=%fused_computation.5 | convolution fusion | flops 605551616 | bytes 3903488 | tf_op jit(solution)/shard_map/while/body/eval_jaxpr/cond/branch_1_fun/pqhe,pke->pqhk/dot_general | solution.py:77
  98.2 0.7 fusion.5
  99.0 2.2 %copy.46 = bf16[1,1,512,576]{3,2,1,0:T(8,128)(2,1)} copy(bf16[1,1,512,576]{2,3,1,0:T(8,128)(2,1)} %copy-done) | data formatting | bytes 1179648 | tf_op jit(solution)/shard_map/while/body/eval_jaxpr/dynamic_slice | solution.py:101
  101.1 2.2 %bitcast_add_fusion = f32[1,64,16,512]{3,2,1,0:T(8,128)S(1)} fusion(f32[1,64,16,512]{3,2,1,0:T(8,128)S(1)} %get-tuple-element.281, bf16[64,16,512]{2,0,1:T(8,128)(2,1)S(1)} %get-tuple-element.353, f32[64,16]{1,0:T(8,128)S(1)} %copy.45, bf16[1,512,576]{2,1,0:T(8,128)(2,1)} %bitcast.98), kind=kOutput, calls=%fused_computation.2 | convolution fusion | flops 537919488 | bytes 5771264 | tf_op jit(solution)/shard_map/while/body/eval_jaxpr/cond/branch_1_fun/pqhk,pkl->pqhl/dot_general | solution.py:85
  106.5 9.0 %conditional.3 = ((f32[1,64,16]{1,2,0:T(8,128)S(1)}, f32[1,64,16]{1,2,0:T(8,128)S(1)}, f32[1,64,16,512]{3,2,1,0:T(8,128)S(1)})) conditional(s32[]{:T(128)} %bitcast.97, (f32[1,64,16]{1,2,0:T(8,128)S(1)}, f32[1,64,16]{1,2,0:T(8,128)S(1)}, f32[1,64,16,512]{3,2,1,0:T(8,128)S(1)}) %tuple.66, (s32[1,512]{1,0:T(1,128)S(1)}, s32[1,1,64]{2,1,0:T(1,128)S(1)}, ...), branch_computations={%region_4.0_spmd, %region_5.7_spmd} | conditional | flops 1146129408 | bytes 17668416 | solution.py:105
  106.5 1.1 constant_dynamic-slice_fusion
  107.7 2.5 %fusion.2 = (f32[64,16]{0,1:T(8,128)S(1)}, f32[512,64,16]{0,1,2:T(8,128)S(1)}) fusion(pred[64,512]{1,0:T(8,128)(4,1)S(1)} %broadcast_compare_fusion, bf16[1,64,16,576]{3,1,2,0:T(8,128)(2,1)} %get-tuple-element.279, bf16[1,1,512,576]{2,3,1,0:T(8,128)(2,1)S(1)} %constant_dynamic-slice_fusion), kind=kOutput, calls=%fused_computation.5 | convolution fusion | flops 605551616 | bytes 3903488 | tf_op jit(solution)/shard_map/while/body/eval_jaxpr/cond/branch_1_fun/pqhe,pke->pqhk/dot_general | solution.py:77
  110.2 0.7 fusion.5
  111.0 2.2 %copy.46 = bf16[1,1,512,576]{3,2,1,0:T(8,128)(2,1)} copy(bf16[1,1,512,576]{2,3,1,0:T(8,128)(2,1)} %copy-done) | data formatting | bytes 1179648 | tf_op jit(solution)/shard_map/while/body/eval_jaxpr/dynamic_slice | solution.py:101
  113.2 2.2 %bitcast_add_fusion = f32[1,64,16,512]{3,2,1,0:T(8,128)S(1)} fusion(f32[1,64,16,512]{3,2,1,0:T(8,128)S(1)} %get-tuple-element.281, bf16[64,16,512]{2,0,1:T(8,128)(2,1)S(1)} %get-tuple-element.353, f32[64,16]{1,0:T(8,128)S(1)} %copy.45, bf16[1,512,576]{2,1,0:T(8,128)(2,1)} %bitcast.98), kind=kOutput, calls=%fused_computation.2 | convolution fusion | flops 537919488 | bytes 5771264 | tf_op jit(solution)/shard_map/while/body/eval_jaxpr/cond/branch_1_fun/pqhk,pkl->pqhl/dot_general | solution.py:85
  118.5 9.0 %conditional.3 = ((f32[1,64,16]{1,2,0:T(8,128)S(1)}, f32[1,64,16]{1,2,0:T(8,128)S(1)}, f32[1,64,16,512]{3,2,1,0:T(8,128)S(1)})) conditional(s32[]{:T(128)} %bitcast.97, (f32[1,64,16]{1,2,0:T(8,128)S(1)}, f32[1,64,16]{1,2,0:T(8,128)S(1)}, f32[1,64,16,512]{3,2,1,0:T(8,128)S(1)}) %tuple.66, (s32[1,512]{1,0:T(1,128)S(1)}, s32[1,1,64]{2,1,0:T(1,128)S(1)}, ...), branch_computations={%region_4.0_spmd, %region_5.7_spmd} | conditional | flops 1146129408 | bytes 17668416 | solution.py:105
  118.5 1.1 constant_dynamic-slice_fusion
  119.8 2.5 %fusion.2 = (f32[64,16]{0,1:T(8,128)S(1)}, f32[512,64,16]{0,1,2:T(8,128)S(1)}) fusion(pred[64,512]{1,0:T(8,128)(4,1)S(1)} %broadcast_compare_fusion, bf16[1,64,16,576]{3,1,2,0:T(8,128)(2,1)} %get-tuple-element.279, bf16[1,1,512,576]{2,3,1,0:T(8,128)(2,1)S(1)} %constant_dynamic-slice_fusion), kind=kOutput, calls=%fused_computation.5 | convolution fusion | flops 605551616 | bytes 3903488 | tf_op jit(solution)/shard_map/while/body/eval_jaxpr/cond/branch_1_fun/pqhe,pke->pqhk/dot_general | solution.py:77
  123.1 2.2 %copy.46 = bf16[1,1,512,576]{3,2,1,0:T(8,128)(2,1)} copy(bf16[1,1,512,576]{2,3,1,0:T(8,128)(2,1)} %copy-done) | data formatting | bytes 1179648 | tf_op jit(solution)/shard_map/while/body/eval_jaxpr/dynamic_slice | solution.py:101
  125.3 2.2 %bitcast_add_fusion = f32[1,64,16,512]{3,2,1,0:T(8,128)S(1)} fusion(f32[1,64,16,512]{3,2,1,0:T(8,128)S(1)} %get-tuple-element.281, bf16[64,16,512]{2,0,1:T(8,128)(2,1)S(1)} %get-tuple-element.353, f32[64,16]{1,0:T(8,128)S(1)} %copy.45, bf16[1,512,576]{2,1,0:T(8,128)(2,1)} %bitcast.98), kind=kOutput, calls=%fused_computation.2 | convolution fusion | flops 537919488 | bytes 5771264 | tf_op jit(solution)/shard_map/while/body/eval_jaxpr/cond/branch_1_fun/pqhk,pkl->pqhl/dot_general | solution.py:85
  130.6 9.1 %conditional.3 = ((f32[1,64,16]{1,2,0:T(8,128)S(1)}, f32[1,64,16]{1,2,0:T(8,128)S(1)}, f32[1,64,16,512]{3,2,1,0:T(8,128)S(1)})) conditional(s32[]{:T(128)} %bitcast.97, (f32[1,64,16]{1,2,0:T(8,128)S(1)}, f32[1,64,16]{1,2,0:T(8,128)S(1)}, f32[1,64,16,512]{3,2,1,0:T(8,128)S(1)}) %tuple.66, (s32[1,512]{1,0:T(1,128)S(1)}, s32[1,1,64]{2,1,0:T(1,128)S(1)}, ...), branch_computations={%region_4.0_spmd, %region_5.7_spmd} | conditional | flops 1146129408 | bytes 17668416 | solution.py:105
  130.6 1.2 constant_dynamic-slice_fusion
  131.9 2.5 %fusion.2 = (f32[64,16]{0,1:T(8,128)S(1)}, f32[512,64,16]{0,1,2:T(8,128)S(1)}) fusion(pred[64,512]{1,0:T(8,128)(4,1)S(1)} %broadcast_compare_fusion, bf16[1,64,16,576]{3,1,2,0:T(8,128)(2,1)} %get-tuple-element.279, bf16[1,1,512,576]{2,3,1,0:T(8,128)(2,1)S(1)} %constant_dynamic-slice_fusion), kind=kOutput, calls=%fused_computation.5 | convolution fusion | flops 605551616 | bytes 3903488 | tf_op jit(solution)/shard_map/while/body/eval_jaxpr/cond/branch_1_fun/pqhe,pke->pqhk/dot_general | solution.py:77
  134.4 0.7 fusion.5
  135.2 2.2 %copy.46 = bf16[1,1,512,576]{3,2,1,0:T(8,128)(2,1)} copy(bf16[1,1,512,576]{2,3,1,0:T(8,128)(2,1)} %copy-done) | data formatting | bytes 1179648 | tf_op jit(solution)/shard_map/while/body/eval_jaxpr/dynamic_slice | solution.py:101
  137.4 2.2 %bitcast_add_fusion = f32[1,64,16,512]{3,2,1,0:T(8,128)S(1)} fusion(f32[1,64,16,512]{3,2,1,0:T(8,128)S(1)} %get-tuple-element.281, bf16[64,16,512]{2,0,1:T(8,128)(2,1)S(1)} %get-tuple-element.353, f32[64,16]{1,0:T(8,128)S(1)} %copy.45, bf16[1,512,576]{2,1,0:T(8,128)(2,1)} %bitcast.98), kind=kOutput, calls=%fused_computation.2 | convolution fusion | flops 537919488 | bytes 5771264 | tf_op jit(solution)/shard_map/while/body/eval_jaxpr/cond/branch_1_fun/pqhk,pkl->pqhl/dot_general | solution.py:85
  142.7 9.1 %conditional.3 = ((f32[1,64,16]{1,2,0:T(8,128)S(1)}, f32[1,64,16]{1,2,0:T(8,128)S(1)}, f32[1,64,16,512]{3,2,1,0:T(8,128)S(1)})) conditional(s32[]{:T(128)} %bitcast.97, (f32[1,64,16]{1,2,0:T(8,128)S(1)}, f32[1,64,16]{1,2,0:T(8,128)S(1)}, f32[1,64,16,512]{3,2,1,0:T(8,128)S(1)}) %tuple.66, (s32[1,512]{1,0:T(1,128)S(1)}, s32[1,1,64]{2,1,0:T(1,128)S(1)}, ...), branch_computations={%region_4.0_spmd, %region_5.7_spmd} | conditional | flops 1146129408 | bytes 17668416 | solution.py:105
  142.7 1.2 constant_dynamic-slice_fusion
  144.0 2.5 %fusion.2 = (f32[64,16]{0,1:T(8,128)S(1)}, f32[512,64,16]{0,1,2:T(8,128)S(1)}) fusion(pred[64,512]{1,0:T(8,128)(4,1)S(1)} %broadcast_compare_fusion, bf16[1,64,16,576]{3,1,2,0:T(8,128)(2,1)} %get-tuple-element.279, bf16[1,1,512,576]{2,3,1,0:T(8,128)(2,1)S(1)} %constant_dynamic-slice_fusion), kind=kOutput, calls=%fused_computation.5 | convolution fusion | flops 605551616 | bytes 3903488 | tf_op jit(solution)/shard_map/while/body/eval_jaxpr/cond/branch_1_fun/pqhe,pke->pqhk/dot_general | solution.py:77
  146.6 0.7 fusion.5
  147.4 2.2 %copy.46 = bf16[1,1,512,576]{3,2,1,0:T(8,128)(2,1)} copy(bf16[1,1,512,576]{2,3,1,0:T(8,128)(2,1)} %copy-done) | data formatting | bytes 1179648 | tf_op jit(solution)/shard_map/while/body/eval_jaxpr/dynamic_slice | solution.py:101
  149.5 2.2 %bitcast_add_fusion = f32[1,64,16,512]{3,2,1,0:T(8,128)S(1)} fusion(f32[1,64,16,512]{3,2,1,0:T(8,128)S(1)} %get-tuple-element.281, bf16[64,16,512]{2,0,1:T(8,128)(2,1)S(1)} %get-tuple-element.353, f32[64,16]{1,0:T(8,128)S(1)} %copy.45, bf16[1,512,576]{2,1,0:T(8,128)(2,1)} %bitcast.98), kind=kOutput, calls=%fused_computation.2 | convolution fusion | flops 537919488 | bytes 5771264 | tf_op jit(solution)/shard_map/while/body/eval_jaxpr/cond/branch_1_fun/pqhk,pkl->pqhl/dot_general | solution.py:85
  154.9 9.0 %conditional.3 = ((f32[1,64,16]{1,2,0:T(8,128)S(1)}, f32[1,64,16]{1,2,0:T(8,128)S(1)}, f32[1,64,16,512]{3,2,1,0:T(8,128)S(1)})) conditional(s32[]{:T(128)} %bitcast.97, (f32[1,64,16]{1,2,0:T(8,128)S(1)}, f32[1,64,16]{1,2,0:T(8,128)S(1)}, f32[1,64,16,512]{3,2,1,0:T(8,128)S(1)}) %tuple.66, (s32[1,512]{1,0:T(1,128)S(1)}, s32[1,1,64]{2,1,0:T(1,128)S(1)}, ...), branch_computations={%region_4.0_spmd, %region_5.7_spmd} | conditional | flops 1146129408 | bytes 17668416 | solution.py:105
  154.9 1.1 constant_dynamic-slice_fusion
  156.1 2.5 %fusion.2 = (f32[64,16]{0,1:T(8,128)S(1)}, f32[512,64,16]{0,1,2:T(8,128)S(1)}) fusion(pred[64,512]{1,0:T(8,128)(4,1)S(1)} %broadcast_compare_fusion, bf16[1,64,16,576]{3,1,2,0:T(8,128)(2,1)} %get-tuple-element.279, bf16[1,1,512,576]{2,3,1,0:T(8,128)(2,1)S(1)} %constant_dynamic-slice_fusion), kind=kOutput, calls=%fused_computation.5 | convolution fusion | flops 605551616 | bytes 3903488 | tf_op jit(solution)/shard_map/while/body/eval_jaxpr/cond/branch_1_fun/pqhe,pke->pqhk/dot_general | solution.py:77
  158.7 0.7 fusion.5
  159.5 2.2 %copy.46 = bf16[1,1,512,576]{3,2,1,0:T(8,128)(2,1)} copy(bf16[1,1,512,576]{2,3,1,0:T(8,128)(2,1)} %copy-done) | data formatting | bytes 1179648 | tf_op jit(solution)/shard_map/while/body/eval_jaxpr/dynamic_slice | solution.py:101
  161.6 2.2 %bitcast_add_fusion = f32[1,64,16,512]{3,2,1,0:T(8,128)S(1)} fusion(f32[1,64,16,512]{3,2,1,0:T(8,128)S(1)} %get-tuple-element.281, bf16[64,16,512]{2,0,1:T(8,128)(2,1)S(1)} %get-tuple-element.353, f32[64,16]{1,0:T(8,128)S(1)} %copy.45, bf16[1,512,576]{2,1,0:T(8,128)(2,1)} %bitcast.98), kind=kOutput, calls=%fused_computation.2 | convolution fusion | flops 537919488 | bytes 5771264 | tf_op jit(solution)/shard_map/while/body/eval_jaxpr/cond/branch_1_fun/pqhk,pkl->pqhl/dot_general | solution.py:85
  166.9 9.0 %conditional.3 = ((f32[1,64,16]{1,2,0:T(8,128)S(1)}, f32[1,64,16]{1,2,0:T(8,128)S(1)}, f32[1,64,16,512]{3,2,1,0:T(8,128)S(1)})) conditional(s32[]{:T(128)} %bitcast.97, (f32[1,64,16]{1,2,0:T(8,128)S(1)}, f32[1,64,16]{1,2,0:T(8,128)S(1)}, f32[1,64,16,512]{3,2,1,0:T(8,128)S(1)}) %tuple.66, (s32[1,512]{1,0:T(1,128)S(1)}, s32[1,1,64]{2,1,0:T(1,128)S(1)}, ...), branch_computations={%region_4.0_spmd, %region_5.7_spmd} | conditional | flops 1146129408 | bytes 17668416 | solution.py:105
  167.0 1.1 constant_dynamic-slice_fusion
  168.2 2.5 %fusion.2 = (f32[64,16]{0,1:T(8,128)S(1)}, f32[512,64,16]{0,1,2:T(8,128)S(1)}) fusion(pred[64,512]{1,0:T(8,128)(4,1)S(1)} %broadcast_compare_fusion, bf16[1,64,16,576]{3,1,2,0:T(8,128)(2,1)} %get-tuple-element.279, bf16[1,1,512,576]{2,3,1,0:T(8,128)(2,1)S(1)} %constant_dynamic-slice_fusion), kind=kOutput, calls=%fused_computation.5 | convolution fusion | flops 605551616 | bytes 3903488 | tf_op jit(solution)/shard_map/while/body/eval_jaxpr/cond/branch_1_fun/pqhe,pke->pqhk/dot_general | solution.py:77
  170.7 0.7 fusion.5
  171.5 2.2 %copy.46 = bf16[1,1,512,576]{3,2,1,0:T(8,128)(2,1)} copy(bf16[1,1,512,576]{2,3,1,0:T(8,128)(2,1)} %copy-done) | data formatting | bytes 1179648 | tf_op jit(solution)/shard_map/while/body/eval_jaxpr/dynamic_slice | solution.py:101
  173.7 2.2 %bitcast_add_fusion = f32[1,64,16,512]{3,2,1,0:T(8,128)S(1)} fusion(f32[1,64,16,512]{3,2,1,0:T(8,128)S(1)} %get-tuple-element.281, bf16[64,16,512]{2,0,1:T(8,128)(2,1)S(1)} %get-tuple-element.353, f32[64,16]{1,0:T(8,128)S(1)} %copy.45, bf16[1,512,576]{2,1,0:T(8,128)(2,1)} %bitcast.98), kind=kOutput, calls=%fused_computation.2 | convolution fusion | flops 537919488 | bytes 5771264 | tf_op jit(solution)/shard_map/while/body/eval_jaxpr/cond/branch_1_fun/pqhk,pkl->pqhl/dot_general | solution.py:85
  179.0 9.0 %conditional.3 = ((f32[1,64,16]{1,2,0:T(8,128)S(1)}, f32[1,64,16]{1,2,0:T(8,128)S(1)}, f32[1,64,16,512]{3,2,1,0:T(8,128)S(1)})) conditional(s32[]{:T(128)} %bitcast.97, (f32[1,64,16]{1,2,0:T(8,128)S(1)}, f32[1,64,16]{1,2,0:T(8,128)S(1)}, f32[1,64,16,512]{3,2,1,0:T(8,128)S(1)}) %tuple.66, (s32[1,512]{1,0:T(1,128)S(1)}, s32[1,1,64]{2,1,0:T(1,128)S(1)}, ...), branch_computations={%region_4.0_spmd, %region_5.7_spmd} | conditional | flops 1146129408 | bytes 17668416 | solution.py:105
  179.0 1.1 constant_dynamic-slice_fusion
  180.2 2.5 %fusion.2 = (f32[64,16]{0,1:T(8,128)S(1)}, f32[512,64,16]{0,1,2:T(8,128)S(1)}) fusion(pred[64,512]{1,0:T(8,128)(4,1)S(1)} %broadcast_compare_fusion, bf16[1,64,16,576]{3,1,2,0:T(8,128)(2,1)} %get-tuple-element.279, bf16[1,1,512,576]{2,3,1,0:T(8,128)(2,1)S(1)} %constant_dynamic-slice_fusion), kind=kOutput, calls=%fused_computation.5 | convolution fusion | flops 605551616 | bytes 3903488 | tf_op jit(solution)/shard_map/while/body/eval_jaxpr/cond/branch_1_fun/pqhe,pke->pqhk/dot_general | solution.py:77
  183.6 2.2 %copy.46 = bf16[1,1,512,576]{3,2,1,0:T(8,128)(2,1)} copy(bf16[1,1,512,576]{2,3,1,0:T(8,128)(2,1)} %copy-done) | data formatting | bytes 1179648 | tf_op jit(solution)/shard_map/while/body/eval_jaxpr/dynamic_slice | solution.py:101
  185.7 2.2 %bitcast_add_fusion = f32[1,64,16,512]{3,2,1,0:T(8,128)S(1)} fusion(f32[1,64,16,512]{3,2,1,0:T(8,128)S(1)} %get-tuple-element.281, bf16[64,16,512]{2,0,1:T(8,128)(2,1)S(1)} %get-tuple-element.353, f32[64,16]{1,0:T(8,128)S(1)} %copy.45, bf16[1,512,576]{2,1,0:T(8,128)(2,1)} %bitcast.98), kind=kOutput, calls=%fused_computation.2 | convolution fusion | flops 537919488 | bytes 5771264 | tf_op jit(solution)/shard_map/while/body/eval_jaxpr/cond/branch_1_fun/pqhk,pkl->pqhl/dot_general | solution.py:85
  188.3 2.4 %fusion.26 = bf16[1,64,16,128]{3,1,2,0:T(8,128)(2,1)S(1)} fusion(bf16[512,16,256]{0,2,1:T(8,128)(2,1)} %bitcast.100, bf16[64,16,512]{2,1,0:T(8,128)(2,1)S(1)} %fusion.30), kind=kOutput, calls=%fused_computation.34 | convolution fusion | flops 134348800 | bytes 3407872 | tf_op jit(solution)/shard_map/pqhl,lhv->pqhv/dot_general | solution.py:109
  190.9 5.7 %fusion.12 = bf16[1,1,64,2048]{3,2,1,0:T(8,128)(2,1)} fusion(bf16[2048,2048]{1,0:T(8,128)(2,1)} %all-gather.5.cloned.1.call-done, bf16[8,8,16,128]{3,2,1,0:T(8,128)(2,1)S(1)} %bitcast.104), kind=kOutput, calls=%fused_computation.24 | convolution fusion | flops 537001984 | bytes 8912896 | tf_op jit(solution)/shard_map/dot_general | solution.py:114
  (123 shorter events, 20.5 us)
Async XLA Ops:
  7.2 16.8 %copy-start.3 = (bf16[1,1,64,576]{3,2,1,0:T(8,128)(2,1)S(1)}, bf16[1,1,64,576]{3,2,1,0:T(8,128)(2,1)}, u32[]{:S(2)}) copy-start(bf16[1,1,64,576]{3,2,1,0:T(8,128)(2,1)} %param.13) | copy-start | bytes 221188
  7.2 16.8 %copy-start.4 = (bf16[512]{0:T(512)(128)(2,1)S(1)}, bf16[512]{0:T(512)(128)(2,1)}, u32[]{:S(2)}) copy-start(bf16[512]{0:T(512)(128)(2,1)} %param.17) | copy-start | bytes 3076
  7.2 68.9 %all-gather.3.cloned.1.call-start = ((), (), s32[]{:S(2)}) async-start(), calls=%async_computation.1 | async-start | bytes 4718592 | tf_op jit(solution)/shard_map/all_gather | solution.py:25
  18.1 172.8 %all-gather.5.cloned.1.call-start = ((), (), s32[]{:S(2)}) async-start(), calls=%async_computation.2 | async-start | bytes 8650752 | tf_op jit(solution)/shard_map/all_gather | solution.py:113
  28.3 8.2 %copy-start.2 = (bf16[1,1,64,3072]{3,2,1,0:T(8,128)(2,1)S(1)}, bf16[1,1,64,3072]{3,2,1,0:T(8,128)(2,1)}, u32[]{:S(2)}) copy-start(bf16[1,1,64,3072]{3,2,1,0:T(8,128)(2,1)} %param.12) | copy-start | bytes 1179652
  28.3 62.6 %all-to-all-start = ((bf16[8,1,1,512,576]{3,4,2,1,0:T(8,128)(2,1)}), bf16[8,1,1,512,576]{3,4,2,1,0:T(8,128)(2,1)}, u32[]{:S(2)}, u32[]{:S(2)}) async-start(bf16[8,1,1,512,576]{3,4,2,1,0:T(8,128)(2,1)} %stack.2), calls=%async_computation | async-start | bytes 9437184 | tf_op jit(solution)/shard_map/all_to_all | solution.py:18
  37.2 2.4 %copy-start.1 = (bf16[1,1,64,16,192]{4,3,2,1,0:T(8,128)(2,1)}, bf16[1,1,64,16,192]{4,3,2,1,0:T(8,128)(2,1)S(1)}, u32[]{:S(2)}) copy-start(bf16[1,1,64,16,192]{4,3,2,1,0:T(8,128)(2,1)S(1)} %reshape.425) | copy-start | bytes 1179652
  76.1 6.5 %slice-start = ((bf16[1,1,64,16,192]{4,3,2,1,0:T(8,128)(2,1)}), bf16[1,1,64,16,128]{4,3,2,1,0:T(8,128)(2,1)S(1)}, s32[]{:S(2)}) async-start(bf16[1,1,64,16,192]{4,3,2,1,0:T(8,128)(2,1)} %copy-done.1), calls=%async_computation.3 | async-start | bytes 524288 | tf_op jit(solution)/shard_map/slice | solution.py:62
  84.6 6.6 %copy-start.5 = (s32[1,8]{1,0:T(1,128)S(1)}, s32[1,8]{1,0:T(1,128)}, u32[]{:S(2)}) copy-start(s32[1,8]{1,0:T(1,128)} %param.16) | copy-start | bytes 100
  95.5 2.7 %copy-start = (bf16[1,1,512,576]{2,3,1,0:T(8,128)(2,1)}, bf16[1,1,512,576]{2,3,1,0:T(8,128)(2,1)S(1)}, u32[]{:S(2)}) copy-start(bf16[1,1,512,576]{2,3,1,0:T(8,128)(2,1)S(1)} %constant_dynamic-slice_fusion) | copy-start | bytes 1769476 | tf_op jit(solution)/shard_map/while/body/eval_jaxpr/cond
  107.6 2.6 %copy-start = (bf16[1,1,512,576]{2,3,1,0:T(8,128)(2,1)}, bf16[1,1,512,576]{2,3,1,0:T(8,128)(2,1)S(1)}, u32[]{:S(2)}) copy-start(bf16[1,1,512,576]{2,3,1,0:T(8,128)(2,1)S(1)} %constant_dynamic-slice_fusion) | copy-start | bytes 1769476 | tf_op jit(solution)/shard_map/while/body/eval_jaxpr/cond
  119.7 2.6 %copy-start = (bf16[1,1,512,576]{2,3,1,0:T(8,128)(2,1)}, bf16[1,1,512,576]{2,3,1,0:T(8,128)(2,1)S(1)}, u32[]{:S(2)}) copy-start(bf16[1,1,512,576]{2,3,1,0:T(8,128)(2,1)S(1)} %constant_dynamic-slice_fusion) | copy-start | bytes 1769476 | tf_op jit(solution)/shard_map/while/body/eval_jaxpr/cond
  131.8 2.6 %copy-start = (bf16[1,1,512,576]{2,3,1,0:T(8,128)(2,1)}, bf16[1,1,512,576]{2,3,1,0:T(8,128)(2,1)S(1)}, u32[]{:S(2)}) copy-start(bf16[1,1,512,576]{2,3,1,0:T(8,128)(2,1)S(1)} %constant_dynamic-slice_fusion) | copy-start | bytes 1769476 | tf_op jit(solution)/shard_map/while/body/eval_jaxpr/cond
  143.9 2.6 %copy-start = (bf16[1,1,512,576]{2,3,1,0:T(8,128)(2,1)}, bf16[1,1,512,576]{2,3,1,0:T(8,128)(2,1)S(1)}, u32[]{:S(2)}) copy-start(bf16[1,1,512,576]{2,3,1,0:T(8,128)(2,1)S(1)} %constant_dynamic-slice_fusion) | copy-start | bytes 1769476 | tf_op jit(solution)/shard_map/while/body/eval_jaxpr/cond
  156.0 2.6 %copy-start = (bf16[1,1,512,576]{2,3,1,0:T(8,128)(2,1)}, bf16[1,1,512,576]{2,3,1,0:T(8,128)(2,1)S(1)}, u32[]{:S(2)}) copy-start(bf16[1,1,512,576]{2,3,1,0:T(8,128)(2,1)S(1)} %constant_dynamic-slice_fusion) | copy-start | bytes 1769476 | tf_op jit(solution)/shard_map/while/body/eval_jaxpr/cond
  168.1 2.6 %copy-start = (bf16[1,1,512,576]{2,3,1,0:T(8,128)(2,1)}, bf16[1,1,512,576]{2,3,1,0:T(8,128)(2,1)S(1)}, u32[]{:S(2)}) copy-start(bf16[1,1,512,576]{2,3,1,0:T(8,128)(2,1)S(1)} %constant_dynamic-slice_fusion) | copy-start | bytes 1769476 | tf_op jit(solution)/shard_map/while/body/eval_jaxpr/cond
  180.1 2.6 %copy-start = (bf16[1,1,512,576]{2,3,1,0:T(8,128)(2,1)}, bf16[1,1,512,576]{2,3,1,0:T(8,128)(2,1)S(1)}, u32[]{:S(2)}) copy-start(bf16[1,1,512,576]{2,3,1,0:T(8,128)(2,1)S(1)} %constant_dynamic-slice_fusion) | copy-start | bytes 1769476 | tf_op jit(solution)/shard_map/while/body/eval_jaxpr/cond
Sparse Core Ops, SparseCore 0:
  18.2 57.8 all-gather.2
  78.7 94.4 all-gather.4
